TPU v7x, 128 devices: a whole 4x4x4 slice. The times are simulated.
128 devices in a mesh: dp: 32 (over z, y_hi, x), tensor: 4 (over y_lo, core).
Axes of the slice: x: 4, y: 4 (y_hi: 2, y_lo: 2; y = y_hi * 2 + y_lo), z: 4, core: 2. Of those that a mesh axis runs over, the one named last changes fastest.
Arguments:
- tokens: bfloat16 [32, 4, 128, 2048], P('dp', 'tensor'), may hold values from -6 to 6
- doc_ids: int32 [32, 4, 128], P('dp'), may hold values from 0 to 3, never falling along the last dimension, each value on 1 to 64 neighbouring positions
- attn_gain: float32 [2048], P(('dp', 'tensor')), may hold values from 0.5 to 1.5
- forget_floor: float32 [2048], P(('dp', 'tensor')), may hold values from 0.5 to 0.98
- w_query: bfloat16 [2048, 2048], P('dp', 'tensor'), may hold values from -0.125 to 0.125
- w_forget: bfloat16 [2048, 2048], P('dp', 'tensor'), may hold values from -0.125 to 0.125
- w_value: bfloat16 [2048, 2048], P('dp', 'tensor'), may hold values from -0.125 to 0.125
- w_outgate: bfloat16 [2048, 2048], P('dp', 'tensor'), may hold values from -0.125 to 0.125
- w_output: bfloat16 [2048, 2048], P('tensor', 'dp'), may hold values from -0.125 to 0.125
- mlp_gain: float32 [2048], P(('dp', 'tensor')), may hold values from 0.5 to 1.5
- w_gate: bfloat16 [2048, 5632], P('dp', 'tensor'), may hold values from -0.125 to 0.125
- w_up: bfloat16 [2048, 5632], P('dp', 'tensor'), may hold values from -0.125 to 0.125
- w_down: bfloat16 [5632, 2048], P('tensor', 'dp'), may hold values from -0.078125 to 0.078125
- cotangent: bfloat16 [32, 4, 128, 2048], P('dp', 'tensor'), may hold values from -6 to 6
Outputs:
- layer_out: bfloat16 [32, 4, 128, 2048], P('dp', 'tensor')
- grad_tokens: float32 [32, 4, 128, 2048], P('dp', 'tensor')
- grad_attn_gain: float32 [2048], P(('dp', 'tensor'))
- grad_floor: float32 [2048], P(('dp', 'tensor'))
- grad_query: float32 [2048, 2048], P('dp', 'tensor')
- grad_forget: float32 [2048, 2048], P('dp', 'tensor')
- grad_value: float32 [2048, 2048], P('dp', 'tensor')
- grad_outgate: float32 [2048, 2048], P('dp', 'tensor')
- grad_output: float32 [2048, 2048], P('tensor', 'dp')
- grad_mlp_gain: float32 [2048], P(('dp', 'tensor'))
- grad_gate: float32 [2048, 5632], P('dp', 'tensor')
- grad_up: float32 [2048, 5632], P('dp', 'tensor')
- grad_down: float32 [5632, 2048], P('tensor', 'dp')
Inputs may be any that keep to these rules, and one draw needn't show every extreme that they name: `doc_ids`: within each row of 128 tokens the sequence numbers never fall; each sequence has 1 to 64 tokens, and the longest has exactly 64.
All inputs are finite; a program needn't handle non-finite values.
Results may differ from a plain program's by a relative error of at most 0.025.
Values may be sent and summed in bfloat16 or wider, within the bound.
No kernel may reach another device: no remote copies, remote signals or barrier semaphores. Data moves between devices by JAX's collectives and lax.ppermute only.
A program may use at most 192 MiB of HBM per device.

v0:
```python
import jax
import jax.numpy as jnp
from jax import lax
from jax.sharding import PartitionSpec as P

HK = 128
BLOCK = 64
epsilon = 1e-06


def row_scale(values):
    return lax.rsqrt(jnp.mean(values * values, axis=-1, keepdims=True) + epsilon)


def silu_slope(values):
    sigmoid_val = jax.nn.sigmoid(values)
    return sigmoid_val * (1.0 + values * (1.0 - sigmoid_val))


def matmul_plain(left, right):
    return jnp.dot(left, right, preferred_element_type=jnp.float32)


def times_trans(left, right):
    return lax.dot_general(
        left, right, (((1,), (1,)), ((), ())), preferred_element_type=jnp.float32
    )


def trans_times(left, right):
    return lax.dot_general(
        left, right, (((0,), (0,)), ((), ())), preferred_element_type=jnp.float32
    )


def recurrence(query, forget_raw, value, floor_vec, doc_row):
    length, heads_n, chan = query.shape
    forget = floor_vec + (1.0 - floor_vec) * jax.nn.sigmoid(forget_raw)
    log_forget = jnp.log(forget)
    keyed = 1.0 - forget
    block_count = length // BLOCK

    def split_blocks(arr):
        return arr.reshape(block_count, BLOCK, heads_n, chan)

    doc_blocks = doc_row.reshape(block_count, BLOCK)
    before = jnp.concatenate([jnp.full((1,), -1, jnp.int32), doc_blocks[:-1, -1]])
    position = jnp.arange(BLOCK)
    causal = position[:, None] >= position[None, :]

    @jax.checkpoint
    def block_step(recurrent_state, pieces):
        query_block, log_b, key_b, value_block, doc_b, prev_doc = pieces
        running_total = jnp.cumsum(log_b, axis=0)
        same_doc = (causal & (doc_b[:, None] == doc_b[None, :]))[:, :, None, None]
        log_gap = running_total[:, None] - running_total[None, :]
        decay = jnp.where(same_doc, jnp.exp(jnp.where(same_doc, log_gap, 0.0)), 0.0)
        scores = jnp.einsum(
            "ihk,jhk,ijhk->ijh", query_block, key_b, decay, precision=lax.Precision.HIGHEST
        )
        intra = jnp.einsum("ijh,jhv->ihv", scores, value_block, precision=lax.Precision.HIGHEST)
        carried_over = (doc_b == prev_doc).astype(jnp.float32)[:, None, None]
        across_blocks = (
            jnp.einsum(
                "bma,maf->bmf",
                query_block * jnp.exp(running_total),
                recurrent_state,
                precision=lax.Precision.HIGHEST,
            )
            * carried_over
        )
        block_finish = running_total[-1]
        end_flag = (doc_b == doc_b[-1]).astype(jnp.float32)[:, None, None]
        weighted_values = key_b * jnp.exp(block_finish[None] - running_total) * end_flag
        carry_marker = (doc_b[-1] == prev_doc).astype(jnp.float32)
        recurrent_state = recurrent_state * (
            jnp.exp(block_finish)[:, :, None] * carry_marker
        ) + jnp.einsum(
            "dmf,dmb->mfb", weighted_values, value_block, precision=lax.Precision.HIGHEST
        )
        return (recurrent_state, intra + across_blocks)

    start_state = jnp.zeros((heads_n, chan, chan), jnp.float32)
    final_state, results = lax.scan(
        block_step,
        start_state,
        (
            split_blocks(query),
            split_blocks(log_forget),
            split_blocks(keyed),
            split_blocks(value),
            doc_blocks,
            before,
        ),
    )
    return results.reshape(length, heads_n, chan)


def row_gather(values):
    count = 4
    spread = jnp.broadcast_to(values[None], (count,) + values.shape)
    got = lax.all_to_all(spread, "tensor", 0, 0, tiled=False)
    return got.reshape((-1,) + values.shape[1:])


def row_sum(values):
    count = 4
    blocks = values.reshape((count, -1) + values.shape[1:])
    got = lax.all_to_all(blocks, "tensor", 0, 0, tiled=False)
    return got.sum(axis=0)


def small_gather(vectors):
    count = 128
    spread = jnp.broadcast_to(vectors[None], (count,) + vectors.shape)
    got = lax.all_to_all(spread, ("dp", "tensor"), 0, 0, tiled=False)
    return jnp.swapaxes(got, 0, 1).reshape(vectors.shape[0], -1)


def small_sum(vectors):
    count = 128
    blocks = vectors.reshape(vectors.shape[0], count, -1)
    got = lax.all_to_all(jnp.swapaxes(blocks, 0, 1), ("dp", "tensor"), 0, 0, tiled=False)
    return got.sum(axis=0)


def shards(
    tokens,
    doc_ids,
    attn_gain,
    forget_floor,
    w_query,
    w_forget,
    w_value,
    w_outgate,
    w_output,
    mlp_gain,
    w_gate,
    w_up,
    w_down,
    cotangent,
):
    gains = small_gather(jnp.stack([attn_gain, forget_floor, mlp_gain]))
    attn_full, floor_full, mlp_full = (gains[0], gains[1], gains[2])
    part_index = lax.axis_index("tensor")
    local_width = w_query.shape[1]
    local_heads = local_width // HK
    hidden_width = w_gate.shape[1]
    floor_local = lax.dynamic_slice_in_dim(
        floor_full, part_index * local_width, local_width
    ).reshape(local_heads, HK)
    model_width = attn_full.shape[0]
    doc_all = doc_ids[0]
    row_count = doc_all.shape[0]
    resid_in = tokens[0].reshape(-1, model_width).astype(jnp.float32)
    cot_local = cotangent[0].reshape(-1, model_width)
    attn_pack = jnp.concatenate([w_query, w_forget, w_value, w_outgate, w_output.T], axis=1)
    mlp_pack = jnp.concatenate([w_gate, w_up, w_down.T], axis=1)
    attn_all = lax.all_gather(attn_pack, "dp", axis=0, tiled=True)
    mlp_all = lax.all_gather(mlp_pack, "dp", axis=0, tiled=True)
    wq_all = attn_all[:, 0 * local_width : 1 * local_width]
    wf_all = attn_all[:, 1 * local_width : 2 * local_width]
    wv_all = attn_all[:, 2 * local_width : 3 * local_width]
    wg_all = attn_all[:, 3 * local_width : 4 * local_width]
    wo_t = attn_all[:, 4 * local_width : 5 * local_width]
    wgate_all = mlp_all[:, 0:hidden_width]
    wup_all = mlp_all[:, hidden_width : 2 * hidden_width]
    wdown_t = mlp_all[:, 2 * hidden_width : 3 * hidden_width]
    scale_one = row_scale(resid_in)
    normed = row_gather((resid_in * scale_one * attn_full).astype(jnp.bfloat16))
    query = matmul_plain(normed, wq_all)
    forget_raw = matmul_plain(normed, wf_all)
    value = matmul_plain(normed, wv_all)
    out_gate = matmul_plain(normed, wg_all)

    def mixer(query_in, forget_in, value_in, floor_in):

        def shaped(arr):
            return arr.reshape(row_count, -1, local_heads, HK)

        mixed_rows = jax.vmap(recurrence, in_axes=(0, 0, 0, None, 0))(
            shaped(query_in), shaped(forget_in), shaped(value_in), floor_in, doc_all
        )
        return mixed_rows.reshape(query_in.shape[0], local_width)

    mixed, pullback = jax.vjp(mixer, query, forget_raw, value, floor_local)
    gate_act = jax.nn.silu(out_gate)
    gated = (mixed * gate_act).astype(jnp.bfloat16)
    branch = row_sum(times_trans(gated, wo_t))
    resid = resid_in + branch
    scale_two = row_scale(resid)
    normed2 = row_gather((resid * scale_two * mlp_full).astype(jnp.bfloat16))
    gate_proj = matmul_plain(normed2, wgate_all)
    up_proj = matmul_plain(normed2, wup_all)
    gate_silu = jax.nn.silu(gate_proj)
    hidden = (gate_silu * up_proj).astype(jnp.bfloat16)
    ffn_out = row_sum(times_trans(hidden, wdown_t))
    layer_out = (resid + ffn_out).astype(jnp.bfloat16).reshape(tokens.shape)
    cot_full = row_gather(cot_local)
    d_hidden = matmul_plain(cot_full, wdown_t)
    grad_down_t = trans_times(cot_full, hidden)
    d_gate = (d_hidden * up_proj * silu_slope(gate_proj)).astype(jnp.bfloat16)
    d_up = (d_hidden * gate_silu).astype(jnp.bfloat16)
    grad_gate = trans_times(normed2, d_gate)
    grad_up = trans_times(normed2, d_up)
    mlp_grads = jnp.concatenate(
        [
            grad_gate.astype(jnp.bfloat16),
            grad_up.astype(jnp.bfloat16),
            grad_down_t.astype(jnp.bfloat16),
        ],
        axis=1,
    )
    mlp_red = lax.psum_scatter(mlp_grads, "dp", scatter_dimension=0, tiled=True).astype(jnp.float32)
    d_normed2 = row_sum(times_trans(d_gate, wgate_all) + times_trans(d_up, wup_all))
    grad_mlp = jnp.sum(d_normed2 * resid * scale_two, axis=0)
    inner_two = jnp.mean(d_normed2 * mlp_full * resid, axis=-1, keepdims=True)
    d_resid = (
        cot_local.astype(jnp.float32)
        + d_normed2 * mlp_full * scale_two
        - resid * scale_two**3 * inner_two
    )
    d_branch = row_gather(d_resid.astype(jnp.bfloat16))
    d_gated = matmul_plain(d_branch, wo_t)
    grad_output_t = trans_times(d_branch, gated)
    d_mixed = d_gated * gate_act
    d_outgate = (d_gated * mixed * silu_slope(out_gate)).astype(jnp.bfloat16)
    d_query, d_forget, d_value, d_floor = pullback(d_mixed)
    d_query = d_query.astype(jnp.bfloat16)
    d_forget = d_forget.astype(jnp.bfloat16)
    d_value = d_value.astype(jnp.bfloat16)
    grad_query = trans_times(normed, d_query)
    grad_forget = trans_times(normed, d_forget)
    grad_value = trans_times(normed, d_value)
    grad_outgate = trans_times(normed, d_outgate)
    attn_grads = jnp.concatenate(
        [
            grad_query.astype(jnp.bfloat16),
            grad_forget.astype(jnp.bfloat16),
            grad_value.astype(jnp.bfloat16),
            grad_outgate.astype(jnp.bfloat16),
            grad_output_t.astype(jnp.bfloat16),
        ],
        axis=1,
    )
    attn_red = lax.psum_scatter(attn_grads, "dp", scatter_dimension=0, tiled=True).astype(
        jnp.float32
    )
    d_normed = row_sum(
        times_trans(d_query, wq_all)
        + times_trans(d_forget, wf_all)
        + times_trans(d_value, wv_all)
        + times_trans(d_outgate, wg_all)
    )
    grad_attn = jnp.sum(d_normed * resid_in * scale_one, axis=0)
    inner_one = jnp.mean(d_normed * attn_full * resid_in, axis=-1, keepdims=True)
    grad_tokens = (
        d_resid + d_normed * attn_full * scale_one - resid_in * scale_one**3 * inner_one
    ).reshape(tokens.shape)
    floor_vector = lax.dynamic_update_slice(
        jnp.zeros((model_width,), jnp.float32), d_floor.reshape(-1), (part_index * local_width,)
    )
    reduced_small = small_sum(jnp.stack([grad_attn, floor_vector, grad_mlp]))
    return (
        layer_out,
        grad_tokens,
        reduced_small[0],
        reduced_small[1],
        attn_red[:, 0 * local_width : 1 * local_width],
        attn_red[:, 1 * local_width : 2 * local_width],
        attn_red[:, 2 * local_width : 3 * local_width],
        attn_red[:, 3 * local_width : 4 * local_width],
        attn_red[:, 4 * local_width : 5 * local_width].T,
        reduced_small[2],
        mlp_red[:, 0:hidden_width],
        mlp_red[:, hidden_width : 2 * hidden_width],
        mlp_red[:, 2 * hidden_width : 3 * hidden_width].T,
    )


def solution(mesh):
    return jax.shard_map(
        shards,
        mesh=mesh,
        in_specs=(
            P("dp", "tensor", None, None),
            P("dp", None, None),
            P(("dp", "tensor")),
            P(("dp", "tensor")),
            P("dp", "tensor"),
            P("dp", "tensor"),
            P("dp", "tensor"),
            P("dp", "tensor"),
            P("tensor", "dp"),
            P(("dp", "tensor")),
            P("dp", "tensor"),
            P("dp", "tensor"),
            P("tensor", "dp"),
            P("dp", "tensor", None, None),
        ),
        out_specs=(
            P("dp", "tensor", None, None),
            P("dp", "tensor", None, None),
            P(("dp", "tensor")),
            P(("dp", "tensor")),
            P("dp", "tensor"),
            P("dp", "tensor"),
            P("dp", "tensor"),
            P("dp", "tensor"),
            P("tensor", "dp"),
            P(("dp", "tensor")),
            P("dp", "tensor"),
            P("dp", "tensor"),
            P("tensor", "dp"),
        ),
        check_vma=False,
    )
```

profile of v0, /device:TPU:0, one launch (start us, length us, event | category | flops | bytes accessed | tf_op | source)
XLA Modules:
  0.0 1291.5 jit_solution(5244657009365066844)
XLA Ops:
  15.7 11.1 all-to-all-start
  47.0 96.4 %all-gather.3.cloned.1.call-done = bf16[2048,2560]{1,0:T(8,128)(2,1)} async-done(((bf16[64,2560]{1,0:T(8,128)(2,1)}), bf16[2048,2560]{1,0:T(8,128)(2,1)}) %all-gather.3.cloned.1.call-update) | async-done | bytes 10485776 | tf_op jit(solution)/shard_map/all_gather | solution.py:159
  174.7 140.9 %while.40 = (s32[]{:T(128)}, f32[4,4,128,128]{3,2,1,0:T(8,128)S(1)}, f32[2,4,64,4,128]{4,2,3,1,0:T(8,128)S(1)}, f32[2,4,4,128,128]{4,3,2,1,0:T(8,128)}, f32[2,4,...) while((s32[]{:T(128)}, ...), condition=%wide.region_3.4_spmd.clone, body=%wide.region_1.3_spmd.clone.sunk | while | flops 563977216 | bytes 88180056 | solution.py:84
  177.3 21.6 %exponential_select_fusion.2 = f32[4,64,64,4,128]{4,3,2,1,0:T(4,128)} fusion(f32[4,64,4,128]{3,2,1,0:T(4,128)S(1)} %fusion.238, pred[4,64,64]{2,1,0:T(8,128)(4,1)S(1)} %compare_and_fusion.4), kind=kLoop, calls=%fused_computation.76.clone.1 | loop fusion | flops 25165824 | bytes 34095104 | tf_op jit(solution)/shard_map/jvp(vmap())/while/body/eval_jaxpr/jit(_where)/select_n | solution.py:57
  200.9 36.4 %fusion.241 = f32[4,64,64,4]{1,2,3,0:T(8,128)S(1)} fusion(f32[4,64,64,4,128]{4,3,2,1,0:T(4,128)} %exponential_select_fusion.2, f32[4,4,128,64]{2,3,1,0:T(8,128)S(1)} %copy.466, f32[4,4,128,64]{2,3,1,0:T(8,128)S(1)} %copy.468), kind=kLoop, calls=%fused_computation.75.clone.1 | loop fusion | flops 25100288 | bytes 34865152 | tf_op jit(solution)/shard_map/jvp(vmap())/while/body/eval_jaxpr/ihk,jhk,ijhk->ijh/dot_general | solution.py:58
  247.5 21.6 %exponential_select_fusion.2 = f32[4,64,64,4,128]{4,3,2,1,0:T(4,128)} fusion(f32[4,64,4,128]{3,2,1,0:T(4,128)S(1)} %fusion.238, pred[4,64,64]{2,1,0:T(8,128)(4,1)S(1)} %compare_and_fusion.4), kind=kLoop, calls=%fused_computation.76.clone.1 | loop fusion | flops 25165824 | bytes 34095104 | tf_op jit(solution)/shard_map/jvp(vmap())/while/body/eval_jaxpr/jit(_where)/select_n | solution.py:57
  271.1 36.4 %fusion.241 = f32[4,64,64,4]{1,2,3,0:T(8,128)S(1)} fusion(f32[4,64,64,4,128]{4,3,2,1,0:T(4,128)} %exponential_select_fusion.2, f32[4,4,128,64]{2,3,1,0:T(8,128)S(1)} %copy.466, f32[4,4,128,64]{2,3,1,0:T(8,128)S(1)} %copy.468), kind=kLoop, calls=%fused_computation.75.clone.1 | loop fusion | flops 25100288 | bytes 34865152 | tf_op jit(solution)/shard_map/jvp(vmap())/while/body/eval_jaxpr/ihk,jhk,ijhk->ijh/dot_general | solution.py:58
  324.3 51.7 %all_to_all.50 = f32[4,128,2048]{2,1,0:T(8,128)} all-to-all(f32[4,128,2048]{2,1,0:T(8,128)S(1)} %bitcast.501), channel_id=1, replica_groups=mesh['dp'=32,'tensor'=4] {'tensor'}, dimensions={0} | all-to-all | bytes 8388608 | tf_op jit(solution)/shard_map/all_to_all | solution.py:109
  385.4 22.6 %all-to-all-done.5 = bf16[4,128,2048]{2,1,0:T(8,128)(2,1)} async-done(((bf16[4,128,2048]{2,1,0:T(8,128)(2,1)}), bf16[4,128,2048]{2,1,0:T(8,128)(2,1)}, u32[]{:S(2)}, u32[]{:S(2)}) %all-to-all-start.5) | async-done | bytes 2097184 | tf_op jit(solution)/shard_map/all_to_all | solution.py:102
  422.3 17.5 %all-to-all-done.3 = bf16[4,128,2048]{2,1,0:T(8,128)(2,1)} async-done(((bf16[4,128,2048]{2,1,0:T(8,128)(2,1)}), bf16[4,128,2048]{2,1,0:T(8,128)(2,1)}, u32[]{:S(2)}, u32[]{:S(2)}) %all-to-all-start.3) | async-done | bytes 2097184 | tf_op jit(solution)/shard_map/all_to_all | solution.py:102
  468.0 51.6 %all_to_all.51 = f32[4,128,2048]{2,1,0:T(8,128)} all-to-all(f32[4,128,2048]{2,1,0:T(8,128)S(1)} %bitcast.513), channel_id=1, replica_groups=mesh['dp'=32,'tensor'=4] {'tensor'}, dimensions={0} | all-to-all | bytes 8388608 | tf_op jit(solution)/shard_map/all_to_all | solution.py:109
  530.6 23.9 %all-to-all-done.7 = bf16[4,128,2048]{2,1,0:T(8,128)(2,1)S(1)} async-done(((bf16[4,128,2048]{2,1,0:T(8,128)(2,1)}), bf16[4,128,2048]{2,1,0:T(8,128)(2,1)S(1)}, u32[]{:S(2)}, u32[]{:S(2)}) %all-to-all-start.7) | async-done | bytes 2097184 | tf_op jit(solution)/shard_map/all_to_all | solution.py:102
  565.6 183.3 %while.41 = (s32[]{:T(128)}, f32[4,4,128,128]{3,2,1,0:T(8,128)}, bf16[2,4,64,4,128]{4,2,3,1,0:T(8,128)(2,1)}, f32[2,4,64,4,128]{4,3,2,1,0:T(4,128)}, f32[2,4,64,...) while((s32[]{:T(128)}, f32[4,4,128,128]{3,2,1,0:T(8,128)}, ...), condition=%wide.region_16.17_spmd.clone, body=%wide.region_9.16_spmd.clone.sunk | while | flops 1228907520 | bytes 80963376 | solution.py:84
  585.8 14.8 %fusion.258 = f32[4,4,128,64]{2,3,1,0:T(8,128)} fusion(f32[4,4,128,64]{2,1,3,0:T(4,128)} %copy.479, f32[4,64,4,128]{3,1,2,0:T(8,128)} %copy-done.12, f32[4,64,4,128]{3,2,1,0:T(4,128)S(1)} %fusion.257, f32[4,64,64,4]{2,3,1,0:T(4,128)} %copy.480, pred[4,64,64]{2,1,0:T(8,128)(4,1)S(1)} %compare_and_fusion.5), kind=kLoop, calls=%fused_computation.3.clone.1 | loop fusion | flops 50200576 | bytes 2375680 | tf_op jit(solution)/shard_map/transpose(jvp(vmap()))/while/body/eval_jaxpr/checkpoint/ihk,jhk,ijhk->ijh/dot_general | solution.py:58
  600.6 14.3 %fusion.259 = f32[4,4,128,64]{2,1,3,0:T(4,128)} fusion(f32[4,4,128,64]{2,3,1,0:T(8,128)S(1)} %bitcast.496, f32[4,64,4,128]{3,1,2,0:T(8,128)S(1)} %copy-done.13, f32[4,64,4,128]{3,2,1,0:T(4,128)S(1)} %fusion.257, f32[4,64,64,4]{2,3,1,0:T(4,128)S(1)} %copy-done.16, pred[4,64,64]{2,1,0:T(8,128)(4,1)S(1)} %compare_and_fusion.5), kind=kLoop, calls=%fused_computation.11.clone.1 | loop fusion | flops 50200576 | bytes 2375680 | tf_op jit(solution)/shard_map/transpose(jvp(vmap()))/while
  622.6 27.4 %fusion.260 = (f32[4,64,4,128]{3,1,2,0:T(8,128)S(1)}, f32[4,64,4,128]{3,2,1,0:T(4,128)}, f32[4,64,64,4]{2,3,1,0:T(4,128)S(1)}) fusion(f32[4,4,128,64]{2,3,1,0:T(8,128)S(1)} %bitcast.497, f32[4,4,128,64]{2,1,3,0:T(4,128)S(1)} %copy-done.15, f32[4,64,4,128]{3,1,2,0:T(8,128)S(1)} %copy-done.14, f32[4,64,4,128]{3,2,1,0:T(4,128)S(1)} %fusion.257, ...), kind=kLoop, calls=%fused_computation.16.clone.1 | loop fusion | flops 100335616 | bytes 3686400 | tf_op jit(solution)/shard_map/transpose(jvp(vmap()))/while/body/eval_jaxpr/checkpoint/reduce_sum | solution.py:56
  677.8 14.8 %fusion.258 = f32[4,4,128,64]{2,3,1,0:T(8,128)} fusion(f32[4,4,128,64]{2,1,3,0:T(4,128)} %copy.479, f32[4,64,4,128]{3,1,2,0:T(8,128)} %copy-done.12, f32[4,64,4,128]{3,2,1,0:T(4,128)S(1)} %fusion.257, f32[4,64,64,4]{2,3,1,0:T(4,128)} %copy.480, pred[4,64,64]{2,1,0:T(8,128)(4,1)S(1)} %compare_and_fusion.5), kind=kLoop, calls=%fused_computation.3.clone.1 | loop fusion | flops 50200576 | bytes 2375680 | tf_op jit(solution)/shard_map/transpose(jvp(vmap()))/while/body/eval_jaxpr/checkpoint/ihk,jhk,ijhk->ijh/dot_general | solution.py:58
  692.6 14.3 %fusion.259 = f32[4,4,128,64]{2,1,3,0:T(4,128)} fusion(f32[4,4,128,64]{2,3,1,0:T(8,128)S(1)} %bitcast.496, f32[4,64,4,128]{3,1,2,0:T(8,128)S(1)} %copy-done.13, f32[4,64,4,128]{3,2,1,0:T(4,128)S(1)} %fusion.257, f32[4,64,64,4]{2,3,1,0:T(4,128)S(1)} %copy-done.16, pred[4,64,64]{2,1,0:T(8,128)(4,1)S(1)} %compare_and_fusion.5), kind=kLoop, calls=%fused_computation.11.clone.1 | loop fusion | flops 50200576 | bytes 2375680 | tf_op jit(solution)/shard_map/transpose(jvp(vmap()))/while
  714.6 27.4 %fusion.260 = (f32[4,64,4,128]{3,1,2,0:T(8,128)S(1)}, f32[4,64,4,128]{3,2,1,0:T(4,128)}, f32[4,64,64,4]{2,3,1,0:T(4,128)S(1)}) fusion(f32[4,4,128,64]{2,3,1,0:T(8,128)S(1)} %bitcast.497, f32[4,4,128,64]{2,1,3,0:T(4,128)S(1)} %copy-done.15, f32[4,64,4,128]{3,1,2,0:T(8,128)S(1)} %copy-done.14, f32[4,64,4,128]{3,2,1,0:T(4,128)S(1)} %fusion.257, ...), kind=kLoop, calls=%fused_computation.16.clone.1 | loop fusion | flops 100335616 | bytes 3686400 | tf_op jit(solution)/shard_map/transpose(jvp(vmap()))/while/body/eval_jaxpr/checkpoint/reduce_sum | solution.py:56
  774.3 13.8 %copy.349 = bf16[2048,2560]{1,0:T(8,128)(2,1)} copy(bf16[2048,2560]{0,1:T(8,128)(2,1)} %fusion.83) | data formatting | bytes 20971520
  811.2 21.2 %copy.351 = bf16[2048,4224]{1,0:T(8,128)(2,1)} copy(bf16[2048,4224]{0,1:T(8,128)(2,1)} %pad_maximum_fusion) | data formatting | bytes 34603008
  859.8 100.0 %all-to-all-done.4 = f32[4,128,2048]{2,1,0:T(8,128)} async-done(((f32[4,128,2048]{2,1,0:T(8,128)}), f32[4,128,2048]{2,1,0:T(8,128)}, u32[]{:S(2)}, u32[]{:S(2)}) %all-to-all-start.4) | async-done | bytes 4194336 | tf_op jit(solution)/shard_map/all_to_all | solution.py:109
  970.1 51.1 %all-to-all-done.8 = f32[4,128,2048]{2,1,0:T(8,128)} async-done(((f32[4,128,2048]{2,1,0:T(8,128)}), f32[4,128,2048]{2,1,0:T(8,128)}, u32[]{:S(2)}, u32[]{:S(2)}) %all-to-all-start.8) | async-done | bytes 4194336 | tf_op jit(solution)/shard_map/all_to_all | solution.py:109
  1054.7 221.6 %reduce-scatter.9.cloned.1.call-done = bf16[64,4224]{1,0:T(8,128)(2,1)} async-done(((bf16[2048,4224]{1,0:T(8,128)(2,1)}), bf16[64,4224]{1,0:T(8,128)(2,1)}) %reduce-scatter.9.cloned.1.call-update) | async-done | bytes 540688
  (401 shorter events, 363.4 us)
Async XLA Ops:
  7.2 136.2 %all-gather.3.cloned.1.call-start = ((), (), s32[]{:S(2)}) async-start(), calls=%async_computation.12 | async-start | bytes 10813440 | tf_op jit(solution)/shard_map/all_gather | solution.py:159
  12.3 401.7 %all-gather.5.cloned.1.call-start = ((), (), s32[]{:S(2)}) async-start(), calls=%async_computation.13 | async-start | bytes 17842176 | tf_op jit(solution)/shard_map/all_gather | solution.py:160
  15.7 23.1 %all-to-all-start = ((f32[128,3,16]{2,1,0:T(4,128)}), f32[128,3,16]{2,1,0:T(4,128)S(1)}, u32[]{:S(2)}, u32[]{:S(2)}) async-start(f32[128,3,16]{2,1,0:T(4,128)} %broadcast_in_dim.179), calls=%async_computation | async-start | bytes 524288 | tf_op jit(solution)/shard_map/all_to_all | solution.py:116
  41.7 109.5 %all-to-all-start.1 = ((bf16[4,128,2048]{2,1,0:T(8,128)(2,1)}), bf16[4,128,2048]{2,1,0:T(8,128)(2,1)}, u32[]{:S(2)}, u32[]{:S(2)}) async-start(bf16[4,128,2048]{2,1,0:T(8,128)(2,1)} %broadcast_in_dim.180), calls=%async_computation.1 | async-start | bytes 4194304 | tf_op jit(solution)/shard_map/all_to_all | solution.py:102
  47.0 104.2 %copy-start.44 = (f32[4,128]{1,0:T(4,128)}, f32[4,128]{1,0:T(4,128)S(1)}, u32[]{:S(2)}) copy-start(f32[4,128]{1,0:T(4,128)S(1)} %get-tuple-element.828) | copy-start | bytes 6148
  47.0 104.2 %copy-start.46 = (f32[4,128]{1,0:T(4,128)}, f32[4,128]{1,0:T(4,128)S(1)}, u32[]{:S(2)}) copy-start(f32[4,128]{1,0:T(4,128)S(1)} %get-tuple-element.829) | copy-start | bytes 6148
  377.6 30.3 %all-to-all-start.5 = ((bf16[4,128,2048]{2,1,0:T(8,128)(2,1)}), bf16[4,128,2048]{2,1,0:T(8,128)(2,1)}, u32[]{:S(2)}, u32[]{:S(2)}) async-start(bf16[4,128,2048]{2,1,0:T(8,128)(2,1)} %broadcast_in_dim.183), calls=%async_computation.5 | async-start | bytes 4194304 | tf_op jit(solution)/shard_map/all_to_all | solution.py:102
  382.3 140.8 %copy-start.39 = (f32[2048]{0:T(1024)}, f32[2048]{0:T(1024)S(1)}, u32[]{:S(2)}) copy-start(f32[2048]{0:T(1024)S(1)} %mul.610) | copy-start | bytes 24580
  384.9 138.2 %copy-start.5 = (f32[128,2048]{1,0:T(8,128)}, f32[128,2048]{1,0:T(8,128)S(1)}, u32[]{:S(2)}) copy-start(f32[128,2048]{1,0:T(8,128)S(1)} %reduce_sum.220) | copy-start | bytes 3145732
  385.2 138.0 %copy-start.48 = (f32[128]{0:T(128)}, f32[128]{0:T(128)S(1)}, u32[]{:S(2)}) copy-start(f32[128]{0:T(128)S(1)} %get-tuple-element.865) | copy-start | bytes 1540
  385.2 138.0 %copy-start.53 = (f32[128]{0:T(128)}, f32[128]{0:T(128)S(1)}, u32[]{:S(2)}) copy-start(f32[128]{0:T(128)S(1)} %get-tuple-element.864) | copy-start | bytes 1540
  409.5 30.2 %all-to-all-start.3 = ((bf16[4,128,2048]{2,1,0:T(8,128)(2,1)}), bf16[4,128,2048]{2,1,0:T(8,128)(2,1)}, u32[]{:S(2)}, u32[]{:S(2)}) async-start(bf16[4,128,2048]{2,1,0:T(8,128)(2,1)} %broadcast_in_dim.181), calls=%async_computation.3 | async-start | bytes 4194304 | tf_op jit(solution)/shard_map/all_to_all | solution.py:102
  525.2 29.3 %all-to-all-start.7 = ((bf16[4,128,2048]{2,1,0:T(8,128)(2,1)}), bf16[4,128,2048]{2,1,0:T(8,128)(2,1)S(1)}, u32[]{:S(2)}, u32[]{:S(2)}) async-start(bf16[4,128,2048]{2,1,0:T(8,128)(2,1)} %broadcast_in_dim.184), calls=%async_computation.7 | async-start | bytes 4194304 | tf_op jit(solution)/shard_map/all_to_all | solution.py:102
  528.8 520.6 %reduce-scatter.7.cloned.1.call-start = ((), (), s32[]{:S(2)}) async-start(), calls=%async_computation.14 | async-start | bytes 10813440
  788.1 488.2 %reduce-scatter.9.cloned.1.call-start = ((), (), s32[]{:S(2)}) async-start(), calls=%async_computation.15 | async-start | bytes 17842176
  841.1 118.7 %all-to-all-start.4 = ((f32[4,128,2048]{2,1,0:T(8,128)}), f32[4,128,2048]{2,1,0:T(8,128)}, u32[]{:S(2)}, u32[]{:S(2)}) async-start(f32[4,128,2048]{2,1,0:T(8,128)} %bitcast.512), calls=%async_computation.4 | async-start | bytes 8388608 | tf_op jit(solution)/shard_map/all_to_all | solution.py:109
  959.7 61.5 %all-to-all-start.8 = ((f32[4,128,2048]{2,1,0:T(8,128)}), f32[4,128,2048]{2,1,0:T(8,128)}, u32[]{:S(2)}, u32[]{:S(2)}) async-start(f32[4,128,2048]{2,1,0:T(8,128)} %bitcast.502), calls=%async_computation.8 | async-start | bytes 8388608 | tf_op jit(solution)/shard_map/all_to_all | solution.py:109
  968.5 68.0 %copy-start.6 = (f32[128,2048]{1,0:T(8,128)S(1)}, f32[128,2048]{1,0:T(8,128)}, u32[]{:S(2)}) copy-start(f32[128,2048]{1,0:T(8,128)} %copy-done.5) | copy-start | bytes 3145732
  968.5 68.0 %copy-start.11 = (f32[128,2048]{1,0:T(8,128)S(1)}, f32[128,2048]{1,0:T(8,128)}, u32[]{:S(2)}) copy-start(f32[128,2048]{1,0:T(8,128)} %copy-done.10) | copy-start | bytes 3145732
  968.5 68.0 %copy-start.22 = (bf16[1,1,128,2048]{3,2,1,0:T(8,128)(2,1)S(1)}, bf16[1,1,128,2048]{3,2,1,0:T(8,128)(2,1)}, u32[]{:S(2)}) copy-start(bf16[1,1,128,2048]{3,2,1,0:T(8,128)(2,1)} %param.31) | copy-start | bytes 1572868
  968.6 68.0 %copy-start.40 = (f32[2048]{0:T(1024)S(1)}, f32[2048]{0:T(1024)}, u32[]{:S(2)}) copy-start(f32[2048]{0:T(1024)} %copy-done.39) | copy-start | bytes 24580
  968.6 68.0 %copy-start.49 = (f32[128]{0:T(128)S(1)}, f32[128]{0:T(128)}, u32[]{:S(2)}) copy-start(f32[128]{0:T(128)} %copy-done.48) | copy-start | bytes 1540
  968.6 68.0 %copy-start.54 = (f32[128]{0:T(128)S(1)}, f32[128]{0:T(128)}, u32[]{:S(2)}) copy-start(f32[128]{0:T(128)} %copy-done.53) | copy-start | bytes 1540
  1027.4 21.3 %all-to-all-start.9 = ((f32[128,3,16]{2,1,0:T(4,128)}), f32[128,3,16]{2,1,0:T(4,128)S(1)}, u32[]{:S(2)}, u32[]{:S(2)}) async-start(f32[128,3,16]{2,1,0:T(4,128)} %copy.307), calls=%async_computation.9 | async-start | bytes 524288 | tf_op jit(solution)/shard_map/all_to_all | solution.py:123
  (67 other events, 833.8 us)
Sparse Core Ops, SparseCore 0:
  12.4 130.9 all-gather.2
  147.0 156.2 all-gather.4
  788.2 207.1 reduce-scatter.6
  1001.1 275.1 reduce-scatter.8
where the time goes:
time: 1300 us; the launch traced here: 1290 us
  waiting for transfers between devices  552 us (42%)
  other arithmetic  280 us (22%)
  matrix products  161 us (12%)
  local copies, waits for them, and re-layouts  130 us (10%)
  blocking collectives  103 us (8%)
  starting transfers between devices  47.8 us (4%)
  between operations  14.8 us (1%)
    unnamed x6, waiting for transfers between devices  222 us
    all_to_all x2, waiting for transfers between devices, row_sum(): got = lax.all_to_all(blocks, 'tensor', 0, 0, tiled=False)  151 us
    all_to_all x2, blocking collectives, row_sum(): got = lax.all_to_all(blocks, 'tensor', 0, 0, tiled=False)  103 us
    dot_general x4, other arithmetic, block_step(): jnp.einsum('ihk,jhk,ijhk->ijh', query_block, key_b, decay, precision=lax....  102 us
    all_gather x1, waiting for transfers between devices, shards(): attn_all = lax.all_gather(attn_pack, 'dp', axis=0, tiled=True)  96.4 us
    all_to_all x4, waiting for transfers between devices, row_gather(): got = lax.all_to_all(spread, 'tensor', 0, 0, tiled=False)  64 us
    unnamed x118, local copies, waits for them, and re-layouts  56.3 us
    reduce_sum x2, other arithmetic, block_step(): log_gap = running_total[:, None] - running_total[None, :]  54.8 us
  transfers between devices with their start and end apart: 12, of which 9 were waited for; matrix products, arithmetic and copies ran while one was open for 23% of the time, Pallas kernels for 0%

commit v1 on v0

--- a/solution.py
+++ b/solution.py
@@ -156,7 +156,10 @@
     cot_local = cotangent[0].reshape(-1, model_width)
     attn_pack = jnp.concatenate([w_query, w_forget, w_value, w_outgate, w_output.T], axis=1)
     mlp_pack = jnp.concatenate([w_gate, w_up, w_down.T], axis=1)
-    attn_all = lax.all_gather(attn_pack, "dp", axis=0, tiled=True)
+    devices = lax.axis_size("dp")
+    parts = jnp.stack([attn_pack for _ in range(devices)])
+    parts = lax.all_to_all(parts, "dp", split_axis=0, concat_axis=0)
+    attn_all = jnp.concatenate(parts, axis=0)
     mlp_all = lax.all_gather(mlp_pack, "dp", axis=0, tiled=True)
     wq_all = attn_all[:, 0 * local_width : 1 * local_width]
     wf_all = attn_all[:, 1 * local_width : 2 * local_width]

time: 1300 us -> 1440 us (1.11)
  waiting for transfers between devices: 552 us -> 664 us
  starting transfers between devices: 47.8 us -> 64.7 us
    all_to_all x0 -> x1, waiting for transfers between devices: none -> 170 us  [shards(): parts = lax.all_to_all(parts, 'dp', split_axis=0, concat_axis=0)]
    all_gather x1 -> x0, waiting for transfers between devices: 96.4 us -> none  [shards(): attn_all = lax.all_gather(attn_pack, 'dp', axis=0, tiled=True)]
    all_to_all x4, waiting for transfers between devices: 64 us -> 87.6 us  [row_gather(): got = lax.all_to_all(spread, 'tensor', 0, 0, tiled=False)]
    all_to_all x2, waiting for transfers between devices: 151 us -> 167 us  [row_sum(): got = lax.all_to_all(blocks, 'tensor', 0, 0, tiled=False)]
    unnamed x6 -> x5, waiting for transfers between devices: 222 us -> 224 us
    unnamed x118 -> x122, local copies, waits for them, and re-layouts: 56.3 us -> 55.3 us
  transfers between devices with their start and end apart: 12 -> 12, of which waited for: 9 -> 10; matrix products, arithmetic and copies ran while one was open for 23% -> 20% of each run, Pallas kernels for 0% -> 0%
where the time goes in v1:
time: 1440 us; the launch traced here: 1430 us
  waiting for transfers between devices  664 us (46%)
  other arithmetic  278 us (19%)
  matrix products  161 us (11%)
  local copies, waits for them, and re-layouts  134 us (9%)
  blocking collectives  103 us (7%)
  starting transfers between devices  64.7 us (4%)
  between operations  15 us (1%)
    unnamed x5, waiting for transfers between devices  224 us
    all_to_all x1, waiting for transfers between devices, shards(): parts = lax.all_to_all(parts, 'dp', split_axis=0, concat_axis=0)  170 us
    all_to_all x2, waiting for transfers between devices, row_sum(): got = lax.all_to_all(blocks, 'tensor', 0, 0, tiled=False)  167 us
    all_to_all x2, blocking collectives, row_sum(): got = lax.all_to_all(blocks, 'tensor', 0, 0, tiled=False)  103 us
    dot_general x4, other arithmetic, block_step(): jnp.einsum('ihk,jhk,ijhk->ijh', query_block, key_b, decay, precision=lax....  102 us
    all_to_all x4, waiting for transfers between devices, row_gather(): got = lax.all_to_all(spread, 'tensor', 0, 0, tiled=False)  87.6 us
    unnamed x122, local copies, waits for them, and re-layouts  55.3 us
    reduce_sum x2, other arithmetic, block_step(): log_gap = running_total[:, None] - running_total[None, :]  54.8 us
  transfers between devices with their start and end apart: 12, of which 10 were waited for; matrix products, arithmetic and copies ran while one was open for 20% of the time, Pallas kernels for 0%

profile of v1, /device:TPU:0, one launch (start us, length us, event | category | flops | bytes accessed | tf_op | source)
XLA Modules:
  0.0 1432.9 jit_solution(4825356464054239457)
XLA Ops:
  43.8 170.4 %all-to-all-done.2 = bf16[32,64,2560]{2,1,0:T(8,128)(2,1)} async-done(((bf16[32,64,2560]{2,1,0:T(8,128)(2,1)}), bf16[32,64,2560]{2,1,0:T(8,128)(2,1)}, u32[]{:S(2)}, u32[]{:S(2)}) %all-to-all-start.2) | async-done | bytes 10485792 | tf_op jit(solution)/shard_map/all_to_all | solution.py:161
  229.2 23.7 %all-to-all-done.1 = bf16[4,128,2048]{2,1,0:T(8,128)(2,1)} async-done(((bf16[4,128,2048]{2,1,0:T(8,128)(2,1)}), bf16[4,128,2048]{2,1,0:T(8,128)(2,1)}, u32[]{:S(2)}, u32[]{:S(2)}) %all-to-all-start.1) | async-done | bytes 2097184 | tf_op jit(solution)/shard_map/all_to_all | solution.py:102
  276.4 151.6 %while.40 = (s32[]{:T(128)}, f32[4,4,128,128]{3,2,1,0:T(8,128)S(1)}, f32[2,4,64,4,128]{4,2,3,1,0:T(8,128)S(1)}, f32[2,4,4,128,128]{4,3,2,1,0:T(8,128)}, f32[2,4,...) while((s32[]{:T(128)}, ...), condition=%wide.region_3.4_spmd.clone, body=%wide.region_1.3_spmd.clone.sunk | while | flops 563977216 | bytes 88180056 | solution.py:84
  279.1 21.6 %exponential_select_fusion.2 = f32[4,64,64,4,128]{4,3,2,1,0:T(4,128)} fusion(f32[4,64,4,128]{3,2,1,0:T(4,128)S(1)} %fusion.238, pred[4,64,64]{2,1,0:T(8,128)(4,1)S(1)} %compare_and_fusion.4), kind=kLoop, calls=%fused_computation.76.clone.1 | loop fusion | flops 25165824 | bytes 34095104 | tf_op jit(solution)/shard_map/jvp(vmap())/while/body/eval_jaxpr/jit(_where)/select_n | solution.py:57
  302.6 36.4 %fusion.241 = f32[4,64,64,4]{1,2,3,0:T(8,128)S(1)} fusion(f32[4,64,64,4,128]{4,3,2,1,0:T(4,128)} %exponential_select_fusion.2, f32[4,4,128,64]{2,3,1,0:T(8,128)S(1)} %copy.464, f32[4,4,128,64]{2,3,1,0:T(8,128)S(1)} %copy.466), kind=kLoop, calls=%fused_computation.75.clone.1 | loop fusion | flops 25100288 | bytes 34865152 | tf_op jit(solution)/shard_map/jvp(vmap())/while/body/eval_jaxpr/ihk,jhk,ijhk->ijh/dot_general | solution.py:58
  349.2 21.6 %exponential_select_fusion.2 = f32[4,64,64,4,128]{4,3,2,1,0:T(4,128)} fusion(f32[4,64,4,128]{3,2,1,0:T(4,128)S(1)} %fusion.238, pred[4,64,64]{2,1,0:T(8,128)(4,1)S(1)} %compare_and_fusion.4), kind=kLoop, calls=%fused_computation.76.clone.1 | loop fusion | flops 25165824 | bytes 34095104 | tf_op jit(solution)/shard_map/jvp(vmap())/while/body/eval_jaxpr/jit(_where)/select_n | solution.py:57
  372.8 36.4 %fusion.241 = f32[4,64,64,4]{1,2,3,0:T(8,128)S(1)} fusion(f32[4,64,64,4,128]{4,3,2,1,0:T(4,128)} %exponential_select_fusion.2, f32[4,4,128,64]{2,3,1,0:T(8,128)S(1)} %copy.464, f32[4,4,128,64]{2,3,1,0:T(8,128)S(1)} %copy.466), kind=kLoop, calls=%fused_computation.75.clone.1 | loop fusion | flops 25100288 | bytes 34865152 | tf_op jit(solution)/shard_map/jvp(vmap())/while/body/eval_jaxpr/ihk,jhk,ijhk->ijh/dot_general | solution.py:58
  436.7 51.7 %all_to_all.55 = f32[4,128,2048]{2,1,0:T(8,128)} all-to-all(f32[4,128,2048]{2,1,0:T(8,128)S(1)} %bitcast.502), channel_id=1, replica_groups=mesh['dp'=32,'tensor'=4] {'tensor'}, dimensions={0} | all-to-all | bytes 8388608 | tf_op jit(solution)/shard_map/all_to_all | solution.py:109
  497.7 22.6 %all-to-all-done.6 = bf16[4,128,2048]{2,1,0:T(8,128)(2,1)} async-done(((bf16[4,128,2048]{2,1,0:T(8,128)(2,1)}), bf16[4,128,2048]{2,1,0:T(8,128)(2,1)}, u32[]{:S(2)}, u32[]{:S(2)}) %all-to-all-start.6) | async-done | bytes 2097184 | tf_op jit(solution)/shard_map/all_to_all | solution.py:102
  534.6 17.5 %all-to-all-done.4 = bf16[4,128,2048]{2,1,0:T(8,128)(2,1)} async-done(((bf16[4,128,2048]{2,1,0:T(8,128)(2,1)}), bf16[4,128,2048]{2,1,0:T(8,128)(2,1)}, u32[]{:S(2)}, u32[]{:S(2)}) %all-to-all-start.4) | async-done | bytes 2097184 | tf_op jit(solution)/shard_map/all_to_all | solution.py:102
  580.2 51.6 %all_to_all.56 = f32[4,128,2048]{2,1,0:T(8,128)} all-to-all(f32[4,128,2048]{2,1,0:T(8,128)S(1)} %bitcast.514), channel_id=1, replica_groups=mesh['dp'=32,'tensor'=4] {'tensor'}, dimensions={0} | all-to-all | bytes 8388608 | tf_op jit(solution)/shard_map/all_to_all | solution.py:109
  642.7 23.9 %all-to-all-done.8 = bf16[4,128,2048]{2,1,0:T(8,128)(2,1)S(1)} async-done(((bf16[4,128,2048]{2,1,0:T(8,128)(2,1)}), bf16[4,128,2048]{2,1,0:T(8,128)(2,1)S(1)}, u32[]{:S(2)}, u32[]{:S(2)}) %all-to-all-start.8) | async-done | bytes 2097184 | tf_op jit(solution)/shard_map/all_to_all | solution.py:102
  677.7 183.1 %while.41 = (s32[]{:T(128)}, f32[4,4,128,128]{3,2,1,0:T(8,128)}, bf16[2,4,64,4,128]{4,2,3,1,0:T(8,128)(2,1)}, f32[2,4,64,4,128]{4,3,2,1,0:T(4,128)}, f32[2,4,64,...) while((s32[]{:T(128)}, f32[4,4,128,128]{3,2,1,0:T(8,128)}, ...), condition=%wide.region_16.17_spmd.clone, body=%wide.region_9.16_spmd.clone.sunk | while | flops 1228907520 | bytes 80963376 | solution.py:84
  698.2 14.8 %fusion.258 = f32[4,4,128,64]{2,3,1,0:T(8,128)} fusion(f32[4,4,128,64]{2,1,3,0:T(4,128)} %copy.477, f32[4,64,4,128]{3,1,2,0:T(8,128)} %copy-done.12, f32[4,64,4,128]{3,2,1,0:T(4,128)S(1)} %fusion.257, f32[4,64,64,4]{2,3,1,0:T(4,128)} %copy.478, pred[4,64,64]{2,1,0:T(8,128)(4,1)S(1)} %compare_and_fusion.5), kind=kLoop, calls=%fused_computation.3.clone.1 | loop fusion | flops 50200576 | bytes 2375680 | tf_op jit(solution)/shard_map/transpose(jvp(vmap()))/while/body/eval_jaxpr/checkpoint/ihk,jhk,ijhk->ijh/dot_general | solution.py:58
  713.0 14.3 fusion.259
  735.0 27.4 %fusion.260 = (f32[4,64,4,128]{3,1,2,0:T(8,128)S(1)}, f32[4,64,4,128]{3,2,1,0:T(4,128)}, f32[4,64,64,4]{2,3,1,0:T(4,128)S(1)}) fusion(f32[4,4,128,64]{2,3,1,0:T(8,128)S(1)} %bitcast.498, f32[4,4,128,64]{2,1,3,0:T(4,128)S(1)} %copy-done.15, f32[4,64,4,128]{3,1,2,0:T(8,128)S(1)} %copy-done.14, f32[4,64,4,128]{3,2,1,0:T(4,128)S(1)} %fusion.257, ...), kind=kLoop, calls=%fused_computation.16.clone.1 | loop fusion | flops 100335616 | bytes 3686400 | tf_op jit(solution)/shard_map/transpose(jvp(vmap()))/while/body/eval_jaxpr/checkpoint/reduce_sum | solution.py:56
  790.1 14.8 %fusion.258 = f32[4,4,128,64]{2,3,1,0:T(8,128)} fusion(f32[4,4,128,64]{2,1,3,0:T(4,128)} %copy.477, f32[4,64,4,128]{3,1,2,0:T(8,128)} %copy-done.12, f32[4,64,4,128]{3,2,1,0:T(4,128)S(1)} %fusion.257, f32[4,64,64,4]{2,3,1,0:T(4,128)} %copy.478, pred[4,64,64]{2,1,0:T(8,128)(4,1)S(1)} %compare_and_fusion.5), kind=kLoop, calls=%fused_computation.3.clone.1 | loop fusion | flops 50200576 | bytes 2375680 | tf_op jit(solution)/shard_map/transpose(jvp(vmap()))/while/body/eval_jaxpr/checkpoint/ihk,jhk,ijhk->ijh/dot_general | solution.py:58
  804.9 14.3 fusion.259
  826.9 27.4 %fusion.260 = (f32[4,64,4,128]{3,1,2,0:T(8,128)S(1)}, f32[4,64,4,128]{3,2,1,0:T(4,128)}, f32[4,64,64,4]{2,3,1,0:T(4,128)S(1)}) fusion(f32[4,4,128,64]{2,3,1,0:T(8,128)S(1)} %bitcast.498, f32[4,4,128,64]{2,1,3,0:T(4,128)S(1)} %copy-done.15, f32[4,64,4,128]{3,1,2,0:T(8,128)S(1)} %copy-done.14, f32[4,64,4,128]{3,2,1,0:T(4,128)S(1)} %fusion.257, ...), kind=kLoop, calls=%fused_computation.16.clone.1 | loop fusion | flops 100335616 | bytes 3686400 | tf_op jit(solution)/shard_map/transpose(jvp(vmap()))/while/body/eval_jaxpr/checkpoint/reduce_sum | solution.py:56
  923.1 21.0 %copy.349 = bf16[2048,4224]{1,0:T(8,128)(2,1)} copy(bf16[2048,4224]{0,1:T(8,128)(2,1)} %pad_maximum_fusion) | data formatting | bytes 34603008
  971.4 109.2 %all-to-all-done.5 = f32[4,128,2048]{2,1,0:T(8,128)} async-done(((f32[4,128,2048]{2,1,0:T(8,128)}), f32[4,128,2048]{2,1,0:T(8,128)}, u32[]{:S(2)}, u32[]{:S(2)}) %all-to-all-start.5) | async-done | bytes 4194336 | tf_op jit(solution)/shard_map/all_to_all | solution.py:109
  1091.1 57.7 %all-to-all-done.9 = f32[4,128,2048]{2,1,0:T(8,128)} async-done(((f32[4,128,2048]{2,1,0:T(8,128)}), f32[4,128,2048]{2,1,0:T(8,128)}, u32[]{:S(2)}, u32[]{:S(2)}) %all-to-all-start.9) | async-done | bytes 4194336 | tf_op jit(solution)/shard_map/all_to_all | solution.py:109
  1155.0 20.6 %all-to-all-start.10 = ((f32[128,3,16]{2,1,0:T(4,128)}), f32[128,3,16]{2,1,0:T(4,128)S(1)}, u32[]{:S(2)}, u32[]{:S(2)}) async-start(f32[128,3,16]{2,1,0:T(4,128)} %copy.305), calls=%async_computation.10 | async-start | bytes 524288 | tf_op jit(solution)/shard_map/all_to_all | solution.py:123
  1194.0 223.6 %reduce-scatter.9.cloned.1.call-done = bf16[64,4224]{1,0:T(8,128)(2,1)} async-done(((bf16[2048,4224]{1,0:T(8,128)(2,1)}), bf16[64,4224]{1,0:T(8,128)(2,1)}) %reduce-scatter.9.cloned.1.call-update) | async-done | bytes 540688
  (405 shorter events, 383.0 us)
Async XLA Ops:
  8.6 21.9 %all-to-all-start = ((f32[128,3,16]{2,1,0:T(4,128)}), f32[128,3,16]{2,1,0:T(4,128)S(1)}, u32[]{:S(2)}, u32[]{:S(2)}) async-start(f32[128,3,16]{2,1,0:T(4,128)} %broadcast_in_dim.179), calls=%async_computation | async-start | bytes 524288 | tf_op jit(solution)/shard_map/all_to_all | solution.py:116
  35.7 178.5 %all-to-all-start.2 = ((bf16[32,64,2560]{2,1,0:T(8,128)(2,1)}), bf16[32,64,2560]{2,1,0:T(8,128)(2,1)}, u32[]{:S(2)}, u32[]{:S(2)}) async-start(bf16[32,64,2560]{2,1,0:T(8,128)(2,1)} %stack.22), calls=%async_computation.2 | async-start | bytes 20971520 | tf_op jit(solution)/shard_map/all_to_all | solution.py:161
  40.8 485.5 %all-gather.2.cloned.1.call-start = ((), (), s32[]{:S(2)}) async-start(), calls=%async_computation.13 | async-start | bytes 17842176 | tf_op jit(solution)/shard_map/all_gather | solution.py:163
  42.0 178.6 %copy-start.54 = (s32[1,4,128]{2,1,0:T(4,128)S(1)}, s32[1,4,128]{2,1,0:T(4,128)}, u32[]{:S(2)}) copy-start(s32[1,4,128]{2,1,0:T(4,128)} %param.19) | copy-start | bytes 6148
  42.5 178.1 %copy-start.52 = (f32[128]{0:T(128)}, f32[128]{0:T(128)S(1)}, u32[]{:S(2)}) copy-start(f32[128]{0:T(128)S(1)} %get-tuple-element.863) | copy-start | bytes 1540
  43.6 176.9 %copy-start.43 = (f32[2048]{0:T(1024)}, f32[2048]{0:T(1024)S(1)}, u32[]{:S(2)}) copy-start(f32[2048]{0:T(1024)S(1)} %mul.601) | copy-start | bytes 24580
  215.8 37.1 %all-to-all-start.1 = ((bf16[4,128,2048]{2,1,0:T(8,128)(2,1)}), bf16[4,128,2048]{2,1,0:T(8,128)(2,1)}, u32[]{:S(2)}, u32[]{:S(2)}) async-start(bf16[4,128,2048]{2,1,0:T(8,128)(2,1)} %broadcast_in_dim.180), calls=%async_computation.1 | async-start | bytes 4194304 | tf_op jit(solution)/shard_map/all_to_all | solution.py:102
  490.0 30.3 %all-to-all-start.6 = ((bf16[4,128,2048]{2,1,0:T(8,128)(2,1)}), bf16[4,128,2048]{2,1,0:T(8,128)(2,1)}, u32[]{:S(2)}, u32[]{:S(2)}) async-start(bf16[4,128,2048]{2,1,0:T(8,128)(2,1)} %broadcast_in_dim.183), calls=%async_computation.6 | async-start | bytes 4194304 | tf_op jit(solution)/shard_map/all_to_all | solution.py:102
  494.6 140.7 %copy-start.38 = (f32[2048]{0:T(1024)}, f32[2048]{0:T(1024)S(1)}, u32[]{:S(2)}) copy-start(f32[2048]{0:T(1024)S(1)} %mul.610) | copy-start | bytes 24580
  497.3 138.1 %copy-start.5 = (f32[128,2048]{1,0:T(8,128)}, f32[128,2048]{1,0:T(8,128)S(1)}, u32[]{:S(2)}) copy-start(f32[128,2048]{1,0:T(8,128)S(1)} %reduce_sum.220) | copy-start | bytes 3145732
  497.5 137.8 %copy-start.50 = (f32[128]{0:T(128)}, f32[128]{0:T(128)S(1)}, u32[]{:S(2)}) copy-start(f32[128]{0:T(128)S(1)} %get-tuple-element.865) | copy-start | bytes 1540
  497.5 137.8 %copy-start.55 = (f32[128]{0:T(128)}, f32[128]{0:T(128)S(1)}, u32[]{:S(2)}) copy-start(f32[128]{0:T(128)S(1)} %get-tuple-element.864) | copy-start | bytes 1540
  521.9 30.2 %all-to-all-start.4 = ((bf16[4,128,2048]{2,1,0:T(8,128)(2,1)}), bf16[4,128,2048]{2,1,0:T(8,128)(2,1)}, u32[]{:S(2)}, u32[]{:S(2)}) async-start(bf16[4,128,2048]{2,1,0:T(8,128)(2,1)} %broadcast_in_dim.181), calls=%async_computation.4 | async-start | bytes 4194304 | tf_op jit(solution)/shard_map/all_to_all | solution.py:102
  637.3 29.3 %all-to-all-start.8 = ((bf16[4,128,2048]{2,1,0:T(8,128)(2,1)}), bf16[4,128,2048]{2,1,0:T(8,128)(2,1)S(1)}, u32[]{:S(2)}, u32[]{:S(2)}) async-start(bf16[4,128,2048]{2,1,0:T(8,128)(2,1)} %broadcast_in_dim.184), calls=%async_computation.8 | async-start | bytes 4194304 | tf_op jit(solution)/shard_map/all_to_all | solution.py:102
  640.9 547.7 %reduce-scatter.7.cloned.1.call-start = ((), (), s32[]{:S(2)}) async-start(), calls=%async_computation.14 | async-start | bytes 10813440
  900.2 517.4 %reduce-scatter.9.cloned.1.call-start = ((), (), s32[]{:S(2)}) async-start(), calls=%async_computation.15 | async-start | bytes 17842176
  952.7 127.9 %all-to-all-start.5 = ((f32[4,128,2048]{2,1,0:T(8,128)}), f32[4,128,2048]{2,1,0:T(8,128)}, u32[]{:S(2)}, u32[]{:S(2)}) async-start(f32[4,128,2048]{2,1,0:T(8,128)} %bitcast.513), calls=%async_computation.5 | async-start | bytes 8388608 | tf_op jit(solution)/shard_map/all_to_all | solution.py:109
  1080.6 68.2 %all-to-all-start.9 = ((f32[4,128,2048]{2,1,0:T(8,128)}), f32[4,128,2048]{2,1,0:T(8,128)}, u32[]{:S(2)}, u32[]{:S(2)}) async-start(f32[4,128,2048]{2,1,0:T(8,128)} %bitcast.503), calls=%async_computation.9 | async-start | bytes 8388608 | tf_op jit(solution)/shard_map/all_to_all | solution.py:109
  1089.5 86.1 %copy-start.6 = (f32[128,2048]{1,0:T(8,128)S(1)}, f32[128,2048]{1,0:T(8,128)}, u32[]{:S(2)}) copy-start(f32[128,2048]{1,0:T(8,128)} %copy-done.5) | copy-start | bytes 3145732
  1089.5 86.1 %copy-start.11 = (f32[128,2048]{1,0:T(8,128)S(1)}, f32[128,2048]{1,0:T(8,128)}, u32[]{:S(2)}) copy-start(f32[128,2048]{1,0:T(8,128)} %copy-done.10) | copy-start | bytes 3145732
  1089.5 86.1 %copy-start.22 = (bf16[1,1,128,2048]{3,2,1,0:T(8,128)(2,1)S(1)}, bf16[1,1,128,2048]{3,2,1,0:T(8,128)(2,1)}, u32[]{:S(2)}) copy-start(bf16[1,1,128,2048]{3,2,1,0:T(8,128)(2,1)} %param.31) | copy-start | bytes 1572868
  1089.5 86.1 %copy-start.39 = (f32[2048]{0:T(1024)S(1)}, f32[2048]{0:T(1024)}, u32[]{:S(2)}) copy-start(f32[2048]{0:T(1024)} %copy-done.38) | copy-start | bytes 24580
  1089.5 86.1 %copy-start.51 = (f32[128]{0:T(128)S(1)}, f32[128]{0:T(128)}, u32[]{:S(2)}) copy-start(f32[128]{0:T(128)} %copy-done.50) | copy-start | bytes 1540
  1155.0 33.0 %all-to-all-start.10 = ((f32[128,3,16]{2,1,0:T(4,128)}), f32[128,3,16]{2,1,0:T(4,128)S(1)}, u32[]{:S(2)}, u32[]{:S(2)}) async-start(f32[128,3,16]{2,1,0:T(4,128)} %copy.305), calls=%async_computation.10 | async-start | bytes 524288 | tf_op jit(solution)/shard_map/all_to_all | solution.py:123
  (69 other events, 994.2 us)
Sparse Core Ops, SparseCore 0:
  45.3 292.6 all-gather.1
  900.3 237.8 reduce-scatter.6
  1144.0 273.5 reduce-scatter.8
